TPU v7x, 32 devices: a whole 2x2x4 slice. The times are simulated.
32 devices in a mesh: groups: 2 (over y), row: 8 (over z, x), col: 2 (over core).
Axes of the slice: x: 2, y: 2, z: 4, core: 2. Of those that a mesh axis runs over, the one named last changes fastest.
Arguments:
- tokens: bfloat16 [1024, 6144], P(('groups', 'row'), 'col'), parts along dimension 0, may hold values from -6 to 6
- w_qkv: bfloat16 [6144, 12288], P('col', 'row'), may hold values from -0.078125 to 0.078125
- query_gain: float32 [128], replicated, may hold values from 0.5 to 1.5
- key_gain: float32 [128], replicated, may hold values from 0.5 to 1.5
- logit_scale: float32 [32], replicated, may hold values from 1 to 3
Outputs:
- attended: bfloat16 [1024, 4096], P(('groups', 'row', 'col')), parts along dimension 0
There are 2 independent parts, one for each index of `groups`. A program takes and returns all parts, laid end to end along the dimension named above; an argument that names none is the same for every part. Nothing has to cross between parts.
All inputs are finite; a program needn't handle non-finite values.
Results may differ from a plain program's by a relative error of at most 0.0091.
Values may be sent and summed in bfloat16 or wider, within the bound.
A program may use at most 128 MiB of HBM per device.

v0:
```python
import math

import jax
import jax.numpy as jnp
from jax import lax
from jax.sharding import PartitionSpec as P


def passed_along(block, axis, distance):
    devices = range(lax.axis_size(axis))
    route = [((i - distance) % len(devices), i) for i in devices]
    return lax.ppermute(block, axis, route)


def rms_scale(values, gain):
    wide = values.astype(jnp.float32)
    power = jnp.mean(wide * wide, axis=-1, keepdims=True)
    return (wide * lax.rsqrt(power + 1e-06) * gain).astype(jnp.bfloat16)


def body(tokens, w_qkv, query_gain, key_gain, logit_scale):
    row_count = lax.axis_size("row")
    half_rows = row_count // 2
    row_rank = lax.axis_index("row")
    side = row_rank // half_rows
    head_group = row_rank % half_rows
    head_dim = query_gain.shape[0]
    half_dim = head_dim // 2
    local_heads = w_qkv.shape[1] // (3 * half_dim)
    tok_rows = tokens.shape[0]
    quarter = tok_rows // 4
    terms = jnp.dot(
        lax.all_gather(tokens, "row", axis=0, tiled=True), w_qkv, preferred_element_type=jnp.float32
    )
    terms = terms.reshape(row_count, 2, tok_rows // 2, -1).transpose(1, 0, 2, 3)
    terms = terms.reshape(2, row_count * (tok_rows // 2), -1)
    mine = lax.psum_scatter(terms, "col", scatter_dimension=0, tiled=True)[0].astype(jnp.bfloat16)
    own_rows = mine.shape[0]
    other = passed_along(mine, "row", half_rows)
    leading = jnp.where(side == 0, mine, other).reshape(own_rows, local_heads, 3, half_dim)
    trailing = jnp.where(side == 0, other, mine).reshape(own_rows, local_heads, 3, half_dim)
    joined = jnp.concatenate([leading, trailing], axis=-1)
    query_normed = rms_scale(joined[:, :, 0], query_gain)
    key_normed = rms_scale(joined[:, :, 1], key_gain)
    keyval = jnp.stack([key_normed, joined[:, :, 2]], axis=2)
    keyval = lax.all_gather(keyval, "col", axis=0, tiled=True)
    key_all = keyval[:, :, 0]
    value_all = keyval[:, :, 1]
    split_queries = query_normed.reshape(row_count, 2, quarter, local_heads, head_dim)
    queries = jnp.where(side == 0, split_queries[:, 0], split_queries[:, 1])
    queries = queries.reshape(row_count * quarter, local_heads, head_dim)
    scales = lax.dynamic_slice_in_dim(logit_scale, head_group * local_heads, local_heads)
    inv_root = 1.0 / math.sqrt(head_dim)
    scores = jnp.einsum("qhd,khd->hqk", queries, key_all, preferred_element_type=jnp.float32)
    scores = scores * (scales * inv_root)[:, None, None]
    expo = jnp.exp(scores)
    probs = (expo / jnp.sum(expo, axis=-1, keepdims=True)).astype(jnp.bfloat16)
    mixed = jnp.einsum("hqk,khd->qhd", probs, value_all, preferred_element_type=jnp.float32).astype(
        jnp.bfloat16
    )
    mixed = mixed.reshape(row_count, quarter, local_heads * head_dim)
    landed = lax.all_to_all(mixed, "row", split_axis=0, concat_axis=0, tiled=True)
    landed = landed.reshape(2, half_rows, quarter, local_heads * head_dim).transpose(0, 2, 1, 3)
    return landed.reshape(2 * quarter, half_rows * local_heads * head_dim)


def solution(mesh):
    in_specs = (P(("groups", "row"), "col"), P("col", "row"), P(), P(), P())
    out_specs = P(("groups", "row", "col"), None)
    return jax.shard_map(body, mesh=mesh, in_specs=in_specs, out_specs=out_specs, check_vma=False)
```

profile of v0, /device:TPU:0, one launch (start us, length us, event | category | flops | bytes accessed | tf_op | source)
XLA Modules:
  0.0 180.0 jit_solution(15504777703538382706)
XLA Ops:
  6.5 0.7 all-gather.3.cloned.1.call-update
  7.3 65.0 %all-gather.3.cloned.1.call-done = bf16[512,3072]{1,0:T(8,128)(2,1)} async-done(((bf16[64,3072]{1,0:T(8,128)(2,1)}), bf16[512,3072]{1,0:T(8,128)(2,1)}) %all-gather.3.cloned.1.call-update) | async-done | bytes 3145744 | tf_op jit(solution)/shard_map/all_gather | solution.py:33
  72.3 8.6 %fusion.11 = f32[512,1536]{1,0:T(8,128)S(1)} fusion(bf16[512,3072]{1,0:T(8,128)(2,1)} %all-gather.3.cloned.1.call-done, bf16[3072,1536]{1,0:T(8,128)(2,1)} %param.6), kind=kOutput, calls=%fused_computation.31 | convolution fusion | flops 4831838208 | bytes 15728640 | tf_op jit(solution)/shard_map/dot_general | solution.py:32
  80.8 1.9 %copy.8 = f32[8,2,32,1536]{3,2,0,1:T(8,128)} copy(f32[8,2,32,1536]{3,2,1,0:T(8,128)S(1)} %bitcast.35) | data formatting | bytes 6291456 | tf_op jit(solution)/shard_map/reshape | solution.py:35
  82.8 9.9 %reduce-scatter.2.cloned.1.call-done = f32[1,256,1536]{2,1,0:T(8,128)} async-done(((f32[2,256,1536]{2,1,0:T(8,128)}), f32[1,256,1536]{2,1,0:T(8,128)}) %reduce-scatter.2.cloned.1.call-update) | async-done | bytes 1572880 | tf_op jit(solution)/shard_map/reduce_scatter | solution.py:37
  92.8 1.6 convert_bitcast_fusion
  94.4 2.8 %collective-permute-start = (bf16[256,1536]{1,0:T(8,128)(2,1)S(1)}, bf16[256,1536]{1,0:T(8,128)(2,1)}, u32[]{:S(2)}, u32[]{:S(2)}) collective-permute-start(bf16[256,1536]{1,0:T(8,128)(2,1)S(1)} %convert_bitcast_fusion), channel_id=1, source_target_pairs={{8,0},{10,2},{12,4},{14,6},{0,8},{2,10},{4,12},{6,14},{9,1},{11,3}... | collective-permute-start | bytes 2359304 | tf_op jit(solution)/shard_map/ppermute | solution.py:12
  97.2 34.9 %collective-permute-done = bf16[256,1536]{1,0:T(8,128)(2,1)} collective-permute-done((bf16[256,1536]{1,0:T(8,128)(2,1)S(1)}, bf16[256,1536]{1,0:T(8,128)(2,1)}, u32[]{:S(2)}, u32[]{:S(2)}) %collective-permute-start) | collective-permute-done | bytes 786464 | tf_op jit(solution)/shard_map/ppermute | solution.py:12
  132.1 1.3 broadcast_select_fusion
  133.4 1.2 copy.9
  134.5 1.8 copy.11
  136.3 1.2 copy.10
  137.5 1.8 copy.12
  139.3 0.3 fusion.6
  139.6 1.5 multiply_reduce_fusion
  141.2 0.3 fusion.4
  141.5 1.1 pad_maximum_fusion
  142.9 0.3 multiply_convert_fusion
  143.3 11.2 %all-gather.5.cloned.1.call-done = bf16[512,8,2,128]{3,0,1,2:T(8,128)(2,1)} async-done(((bf16[256,8,2,128]{3,0,1,2:T(8,128)(2,1)}), bf16[512,8,2,128]{3,0,1,2:T(8,128)(2,1)}) %all-gather.5.cloned.1.call-update) | async-done | bytes 2097168 | tf_op jit(solution)/shard_map/all_gather | solution.py:46
  154.4 1.9 %fusion = (f32[8,128]{1,0:T(8,128)S(1)}, f32[8,128,512]{2,1,0:T(8,128)S(1)}) fusion(f32[8]{0:T(128)S(1)} %dynamic-slice_multiply_fusion, bf16[128,8,128]{2,0,1:T(8,128)(2,1)S(1)} %bitcast.38, bf16[512,8,2,128]{3,0,1,2:T(8,128)(2,1)} %all-gather.5.cloned.1.call-done), kind=kOutput, calls=%fused_computation.2 | convolution fusion | flops 135265280 | bytes 3412000 | tf_op jit(solution)/shard_map/qhd,khd->hqk/dot_general | solution.py:54
  156.4 0.8 fusion.1
  157.5 14.9 %all_to_all.5 = bf16[8,16,1024]{2,1,0:T(8,128)(2,1)S(1)} all-to-all(bf16[8,16,1024]{2,1,0:T(8,128)(2,1)S(1)} %reshape.67), channel_id=1, replica_groups=mesh['groups'=2,'row'=8,'col'=2] {'row'}, dimensions={0} | all-to-all | bytes 524288 | tf_op jit(solution)/shard_map/all_to_all | solution.py:62
  172.4 0.2 copy.15
  172.6 0.8 copy.17
  (24 shorter events, 0.7 us)
Async XLA Ops:
  6.5 65.7 %all-gather.3.cloned.1.call-start = ((), (), s32[]{:S(2)}) async-start(), calls=%async_computation.2 | async-start | bytes 3538944 | tf_op jit(solution)/shard_map/all_gather | solution.py:33
  7.3 85.5 %reduce-scatter.2.cloned.1.call-start = ((), (), s32[]{:S(2)}) async-start(), calls=%async_computation.3 | async-start | bytes 4718592 | tf_op jit(solution)/shard_map/reduce_scatter | solution.py:37
  82.8 71.6 %all-gather.5.cloned.1.call-start = ((), (), s32[]{:S(2)}) async-start(), calls=%async_computation.4 | async-start | bytes 3145728 | tf_op jit(solution)/shard_map/all_gather | solution.py:46
  92.8 39.3 %copy-start = (f32[1,256,1536]{2,1,0:T(8,128)S(1)}, f32[1,256,1536]{2,1,0:T(8,128)}, u32[]{:S(2)}) copy-start(f32[1,256,1536]{2,1,0:T(8,128)} %reduce-scatter.2.cloned.1.call-done) | copy-start | bytes 4718596
  94.4 37.7 %collective-permute-start = (bf16[256,1536]{1,0:T(8,128)(2,1)S(1)}, bf16[256,1536]{1,0:T(8,128)(2,1)}, u32[]{:S(2)}, u32[]{:S(2)}) collective-permute-start(bf16[256,1536]{1,0:T(8,128)(2,1)S(1)} %convert_bitcast_fusion), channel_id=1, source_target_pairs={{8,0},{10,2},{12,4},{14,6},{0,8},{2,10},{4,12},{6,14},{9,1},{11,3}... | collective-permute-start | bytes 2359304 | tf_op jit(solution)/shard_map/ppermute | solution.py:12
  139.6 1.6 copy-start.3
  141.1 1.5 copy-start.5
  141.1 1.7 copy-start.1
  141.1 1.7 copy-start.4
  154.4 1.9 %copy-start.2 = (bf16[512,8,2,128]{3,0,1,2:T(8,128)(2,1)S(1)}, bf16[512,8,2,128]{3,0,1,2:T(8,128)(2,1)}, u32[]{:S(2)}) copy-start(bf16[512,8,2,128]{3,0,1,2:T(8,128)(2,1)} %all-gather.5.cloned.1.call-done) | copy-start | bytes 6291460
Sparse Core Ops, SparseCore 0:
  9.5 62.7 all-gather.2
  82.9 9.8 reduce-scatter.1
  142.7 11.6 all-gather.4
where the time goes:
time: 180 us
  waiting for transfers between devices  122 us (68%)
  blocking collectives  14.9 us (8%)
  between operations  13.3 us (7%)
  matrix products  11.3 us (6%)
  local copies, waits for them, and re-layouts  9.25 us (5%)
  other arithmetic  6.59 us (4%)
  starting transfers between devices  2.92 us (2%)
    all_gather x1, waiting for transfers between devices, body(): lax.all_gather(tokens, 'row', axis=0, tiled=True)  65 us
    ppermute x1, waiting for transfers between devices, passed_along(): return lax.ppermute(block, axis, route)  34.9 us
    all_to_all x1, blocking collectives, body(): lax.all_to_all(mixed, 'row', split_axis=0, concat_axis=0, tiled=True)  14.9 us
    all_gather x1, waiting for transfers between devices, body(): keyval = lax.all_gather(keyval, 'col', axis=0, tiled=True)  11.2 us
    reduce_scatter x1, waiting for transfers between devices, body(): lax.psum_scatter(terms, 'col', scatter_dimension=0, tiled=True)[0]  9.94 us
    dot_general x1, matrix products, body(): jnp.dot(lax.all_gather(tokens, 'row', axis=0, tiled=True), w_qkv, preferr...  8.56 us
  transfers between devices with their start and end apart: 4, of which 4 were waited for; matrix products, arithmetic and copies ran while one was open for 0% of the time, Pallas kernels for 0%

commit v1 on v0

--- a/solution.py
+++ b/solution.py
@@ -1,9 +1,318 @@
+import functools
 import math
 
 import jax
 import jax.numpy as jnp
 from jax import lax
+from jax.experimental import pallas as pl
+from jax.experimental.pallas import tpu as pltpu
 from jax.sharding import PartitionSpec as P
+
+MESH = pl.DeviceIdType.MESH
+FAST = 2
+TILE = 256
+
+
+def visit_order(depth):
+    return [sorted(range(depth), key=lambda other: (abs(other - z), other)) for z in range(depth)]
+
+
+def pick(index, values):
+    chosen = jnp.int32(values[0])
+    for i, value in enumerate(values[1:], 1):
+        chosen = jnp.where(index == i, jnp.int32(value), chosen)
+    return chosen
+
+
+def fused_kernel(
+    row_count, local_heads, head_dim,
+    tokens, w_qkv, query_gain, key_gain, logit_scale, out,
+    toks, weights, part_out, part_in, acc, joined, crossing, qn, kn, vv, att,
+    own_sem, w_sem, gather_send, gather_recv, part_send, part_recv,
+    cross_send, cross_recv, out_send, out_recv, self_sem,
+):
+    depth = row_count // FAST
+    half_rows = row_count // 2
+    half_dim = head_dim // 2
+    heads = local_heads // 4
+    span = heads * 3 * half_dim
+    tok_rows = tokens.shape[0]
+    slab = FAST * tok_rows
+    out_rows = tok_rows // 2
+    order = visit_order(depth)
+
+    row = lax.axis_index("row")
+    col = lax.axis_index("col")
+    z = row // FAST
+    x = lax.rem(row, FAST)
+    side = row // half_rows
+    group = lax.rem(row, half_rows)
+    other_col = 1 - col
+    other_row = lax.rem(row + half_rows, row_count)
+    across = z * FAST + (1 - x)
+    me = row * 2 + col
+
+    def w_copy(dest_col, far):
+        dest_side = side if far == 0 else 1 - side
+        mine = 0 if dest_col is other_col else 1
+        start = pl.multiple_of((dest_side * 2 + dest_col) * span, 128)
+        return pltpu.make_async_copy(
+            w_qkv.at[:, pl.ds(start, span)],
+            weights.at[:, pl.ds((mine * 2 + far) * span, span)],
+            w_sem.at[mine * 2 + far],
+        )
+
+    w_copies = [w_copy(c, far) for c in (other_col, col) for far in (0, 1)]
+    own_copy = pltpu.make_async_copy(
+        tokens, toks.at[pl.ds(pl.multiple_of(row * tok_rows, tok_rows), tok_rows)], own_sem
+    )
+    own_copy.start()
+
+    barrier = pltpu.get_barrier_semaphore()
+    for step in range(row_count):
+        for c in (0, 1):
+            if step == 0 and c == 0:
+                continue
+            peer = lax.rem(row + step, row_count)
+            pl.semaphore_signal(
+                barrier, inc=1,
+                device_id={"row": peer, "col": col if c == 0 else other_col},
+                device_id_type=MESH,
+            )
+    pl.semaphore_wait(barrier, 2 * row_count - 1)
+
+    def block_at(block):
+        return toks.at[pl.ds(pl.multiple_of(block * tok_rows, tok_rows), tok_rows)]
+
+    def gather_copy(block, way, target, source=None):
+        return pltpu.make_async_remote_copy(
+            src_ref=block_at(block) if source is None else source,
+            dst_ref=block_at(block),
+            send_sem=gather_send.at[way, block],
+            recv_sem=gather_recv.at[block],
+            device_id={"row": target},
+            device_id_type=MESH,
+        )
+
+    def column(distance, act):
+        for sign in (0,) if distance == 0 else (-1, 1):
+            at = z + sign * distance
+            block = at * FAST + x
+            source = tokens if distance == 0 else None
+
+            @pl.when(jnp.logical_and(at >= 0, at < depth))
+            def _():
+                if act == "start" and distance:
+                    gather_copy(block, 0, across).wait_recv()
+
+                def go(copy):
+                    if act == "start":
+                        copy.start()
+                    else:
+                        copy.wait_send()
+
+                if sign <= 0:
+
+                    @pl.when(z + 1 < depth)
+                    def _():
+                        go(gather_copy(block, 1, row + FAST, source))
+
+                if sign >= 0:
+
+                    @pl.when(z >= 1)
+                    def _():
+                        go(gather_copy(block, 2, row - FAST, source))
+
+                go(gather_copy(block, 0, across, source))
+
+    def part_copy(k):
+        return pltpu.make_async_remote_copy(
+            src_ref=part_out.at[k], dst_ref=part_in.at[k],
+            send_sem=part_send.at[k], recv_sem=part_recv.at[k],
+            device_id={"col": other_col}, device_id_type=MESH,
+        )
+
+    def slab_of(at):
+        return pl.ds(pl.multiple_of(at * slab, slab), slab)
+
+    def cross_copy(k, at):
+        return pltpu.make_async_remote_copy(
+            src_ref=crossing.at[k], dst_ref=joined.at[side, slab_of(at)],
+            send_sem=cross_send.at[k], recv_sem=cross_recv.at[at],
+            device_id={"row": other_row}, device_id_type=MESH,
+        )
+
+    def batch(k):
+        at = pick(z, [seq[k] for seq in order])
+        gather_copy(at * FAST + (1 - x), 0, across).wait_recv()
+        if k == 0:
+            own_copy.wait()
+            for copy in w_copies:
+                copy.wait()
+        rows = slab_of(at)
+        tiles = 2 * span // TILE
+
+        @pl.loop(0, tiles)
+        def _(n):
+            part_out[k, :, pl.ds(pl.multiple_of(n * TILE, TILE), TILE)] = jnp.dot(
+                toks[rows, :], weights[:, pl.ds(pl.multiple_of(n * TILE, TILE), TILE)],
+                preferred_element_type=jnp.float32,
+            )
+
+        part_copy(k).start()
+
+        @pl.loop(0, tiles)
+        def _(n):
+            acc[:, pl.ds(pl.multiple_of(n * TILE, TILE), TILE)] = jnp.dot(
+                toks[rows, :], weights[:, pl.ds(pl.multiple_of(2 * span + n * TILE, TILE), TILE)],
+                preferred_element_type=jnp.float32,
+            )
+
+        part_copy(k).wait_recv()
+        crossing[k] = (acc[:, span:] + part_in[k, :, span:]).astype(jnp.bfloat16)
+        cross_copy(k, at).start()
+        joined[side, rows, :] = (acc[:, :span] + part_in[k, :, :span]).astype(jnp.bfloat16)
+
+    column(0, "start")
+    for copy in w_copies:
+        copy.start()
+    column(1, "start")
+    for k in range(depth):
+        batch(k)
+        if k + 2 < depth:
+            column(k + 2, "start")
+
+    lanes = lax.broadcasted_iota(jnp.int32, (slab, head_dim), 1)
+    low = lanes < half_dim
+
+    def prepare(at):
+        pltpu.make_async_remote_copy(
+            src_ref=crossing.at[0], dst_ref=joined.at[1 - side, slab_of(at)],
+            send_sem=cross_send.at[0], recv_sem=cross_recv.at[at],
+            device_id={"row": other_row}, device_id_type=MESH,
+        ).wait_recv()
+        rows = slab_of(at)
+
+        def pair(piece):
+            first = joined[0, rows, piece * head_dim:(piece + 1) * head_dim].astype(jnp.float32)
+            second = joined[1, rows, piece * head_dim:(piece + 1) * head_dim].astype(jnp.float32)
+            return (
+                jnp.where(low, first, pltpu.roll(second, half_dim, 1)),
+                jnp.where(low, pltpu.roll(first, half_dim, 1), second),
+            )
+
+        def normed(wide, gain):
+            power = jnp.mean(wide * wide, axis=-1, keepdims=True)
+            return (wide * lax.rsqrt(power + 1e-06) * gain[...]).astype(jnp.bfloat16)
+
+        for j in range(heads // 2):
+            parts = [part for piece in range(3) for part in pair(3 * j + piece)]
+            for i in range(2):
+                query, key, value = parts[3 * i:3 * i + 3]
+                qn[2 * j + i, rows, :] = normed(query, query_gain)
+                kn[2 * j + i, rows, :] = normed(key, key_gain)
+                vv[2 * j + i, rows, :] = value.astype(jnp.bfloat16)
+
+    for k in range(depth):
+        prepare(pick(z, [seq[k] for seq in order]))
+
+    first_head = group * local_heads + (side * 2 + col) * heads
+    out_cols = pl.ds(pl.multiple_of(first_head * head_dim, heads * head_dim), heads * head_dim)
+    inv_root = 1.0 / math.sqrt(head_dim)
+
+    def out_copies(at, act):
+        for xx in range(FAST):
+            for cc in (0, 1):
+                target = at * FAST + xx
+                source = att.at[
+                    pl.ds(pl.multiple_of(target * tok_rows + cc * out_rows, out_rows), out_rows)
+                ]
+                is_me = jnp.logical_and(target == row, col == cc)
+
+                @pl.when(is_me)
+                def _():
+                    copy = pltpu.make_async_copy(source, out.at[:, out_cols], self_sem)
+                    copy.start() if act == "start" else copy.wait()
+
+                @pl.when(jnp.logical_not(is_me))
+                def _():
+                    copy = pltpu.make_async_remote_copy(
+                        src_ref=source, dst_ref=out.at[:, out_cols],
+                        send_sem=out_send.at[target * 2 + cc], recv_sem=out_recv.at[me],
+                        device_id={"row": target, "col": jnp.int32(cc)}, device_id_type=MESH,
+                    )
+                    copy.start() if act == "start" else copy.wait_send()
+
+    for k in reversed(range(depth)):
+        at = pick(z, [seq[k] for seq in order])
+        rows = slab_of(at)
+        for i in range(heads):
+            scores = lax.dot_general(
+                qn[i, rows, :], kn[i], (((1,), (1,)), ((), ())), preferred_element_type=jnp.float32
+            )
+            expo = jnp.exp(scores * (logit_scale[first_head + i] * inv_root))
+            probs = (expo / jnp.sum(expo, axis=-1, keepdims=True)).astype(jnp.bfloat16)
+            att[rows, i * head_dim:(i + 1) * head_dim] = jnp.dot(
+                probs, vv[i], preferred_element_type=jnp.float32
+            ).astype(jnp.bfloat16)
+        out_copies(at, "start")
+
+    for distance in range(depth):
+        column(distance, "finish")
+    for k in range(depth):
+        part_copy(k).wait_send()
+        cross_copy(k, pick(z, [seq[k] for seq in order])).wait_send()
+    for at in range(depth):
+        out_copies(at, "finish")
+    for source in range(2 * row_count):
+
+        @pl.when(source != me)
+        def _():
+            pltpu.make_async_remote_copy(
+                src_ref=att.at[pl.ds(0, out_rows)], dst_ref=out.at[:, out_cols],
+                send_sem=out_send.at[source], recv_sem=out_recv.at[source],
+                device_id={"row": other_row}, device_id_type=MESH,
+            ).wait_recv()
+
+
+def fused(tokens, w_qkv, query_gain, key_gain, logit_scale):
+    row_count = lax.axis_size("row")
+    head_dim = query_gain.shape[0]
+    local_heads = w_qkv.shape[1] // (3 * (head_dim // 2))
+    heads = local_heads // 4
+    span = w_qkv.shape[1] // 4
+    tok_rows, width = tokens.shape
+    count = tok_rows * row_count
+    depth = row_count // FAST
+    slab = FAST * tok_rows
+    vmem, hbm = pl.BlockSpec(memory_space=pltpu.VMEM), pl.BlockSpec(memory_space=pl.ANY)
+    dma = pltpu.SemaphoreType.DMA
+    half = jnp.bfloat16
+    return pl.pallas_call(
+        functools.partial(fused_kernel, row_count, local_heads, head_dim),
+        out_shape=jax.ShapeDtypeStruct((tok_rows // 2, row_count // 2 * local_heads * head_dim), half),
+        in_specs=[hbm, hbm, vmem, vmem, pl.BlockSpec(memory_space=pltpu.SMEM)],
+        out_specs=vmem,
+        scratch_shapes=[
+            pltpu.VMEM((count, width), half),
+            pltpu.VMEM(w_qkv.shape, half),
+            pltpu.VMEM((depth, slab, 2 * span), jnp.float32),
+            pltpu.VMEM((depth, slab, 2 * span), jnp.float32),
+            pltpu.VMEM((slab, 2 * span), jnp.float32),
+            pltpu.VMEM((2, count, span), half),
+            pltpu.VMEM((depth, slab, span), half),
+            pltpu.VMEM((heads, count, head_dim), half),
+            pltpu.VMEM((heads, count, head_dim), half),
+            pltpu.VMEM((heads, count, head_dim), half),
+            pltpu.VMEM((count, heads * head_dim), half),
+            dma, dma((4,)), dma((3, row_count)), dma((row_count,)), dma((depth,)), dma((depth,)),
+            dma((depth,)), dma((depth,)), dma((2 * row_count,)), dma((2 * row_count,)), dma,
+        ],
+        compiler_params=pltpu.CompilerParams(
+            collective_id=0, has_side_effects=True, vmem_limit_bytes=60 * 2**20
+        ),
+        name="fused_attention",
+    )(tokens, w_qkv, query_gain.reshape(1, -1), key_gain.reshape(1, -1), logit_scale)
 
 
 def passed_along(block, axis, distance):
@@ -64,7 +373,26 @@
     return landed.reshape(2 * quarter, half_rows * local_heads * head_dim)
 
 
+def fits(mesh, head_dim, columns):
+    row_count = mesh.shape["row"]
+    local_heads = columns // row_count // (3 * (head_dim // 2))
+    span = columns // row_count // 4
+    return (
+        mesh.shape["col"] == 2
+        and row_count % (2 * FAST) == 0
+        and head_dim % 128 == 0
+        and local_heads % 8 == 0
+        and 2 * span % TILE == 0
+    )
+
+
 def solution(mesh):
     in_specs = (P(("groups", "row"), "col"), P("col", "row"), P(), P(), P())
     out_specs = P(("groups", "row", "col"), None)
-    return jax.shard_map(body, mesh=mesh, in_specs=in_specs, out_specs=out_specs, check_vma=False)
+
+    def run(tokens, w_qkv, query_gain, key_gain, logit_scale):
+        inner = fused if fits(mesh, query_gain.shape[0], w_qkv.shape[1]) else body
+        placed = jax.shard_map(inner, mesh=mesh, in_specs=in_specs, out_specs=out_specs, check_vma=False)
+        return placed(tokens, w_qkv, query_gain, key_gain, logit_scale)
+
+    return run

time: 180 us -> 67.9 us (0.38)
  waiting for transfers between devices: 122 us -> 0 us
  Pallas kernels: 0 us -> 66.1 us
  blocking collectives: 14.9 us -> 0 us
  between operations: 13.3 us -> 0.01 us
  matrix products: 11.3 us -> 0 us
  local copies, waits for them, and re-layouts: 9.25 us -> 1.67 us
  other arithmetic: 6.59 us -> 0 us
  starting transfers between devices: 2.92 us -> 0 us
    all_gather x2 -> x0, waiting for transfers between devices: 76.1 us -> none  [the longest x1 65 us: body(): lax.all_gather(tokens, 'row', axis=0, tiled=True)]
    pallas_call x0 -> x1, Pallas kernels: none -> 66.1 us  [fused(): pl.pallas_call(functools.partial(fused_kernel, row_count, local_heads, he...]
    ppermute x1 -> x0, waiting for transfers between devices: 34.9 us -> none  [passed_along(): return lax.ppermute(block, axis, route)]
    all_to_all x1 -> x0, blocking collectives: 14.9 us -> none  [body(): lax.all_to_all(mixed, 'row', split_axis=0, concat_axis=0, tiled=True)]
    dot_general x3 -> x0, matrix products: 11.3 us -> none  [the longest x1 8.56 us: body(): jnp.dot(lax.all_gather(tokens, 'row', axis=0, tiled=True), w_qkv, preferr...]
    reduce_scatter x1 -> x0, waiting for transfers between devices: 9.94 us -> none  [body(): lax.psum_scatter(terms, 'col', scatter_dimension=0, tiled=True)[0]]
    reshape x4 -> x0, local copies, waits for them, and re-layouts: 5.59 us -> none  [the longest x1 1.92 us: body(): terms = terms.reshape(row_count, 2, tok_rows // 2, -1).transpose(1, 0, 2, 3)]
    ppermute x1 -> x0, starting transfers between devices: 2.84 us -> none  [passed_along(): return lax.ppermute(block, axis, route)]
  transfers between devices with their start and end apart: 4 -> 0, of which waited for: 4 -> 0; matrix products, arithmetic and copies ran while one was open for 0% -> 0% of each run, Pallas kernels for 0% -> 0%
where the time goes in v1:
time: 67.9 us; the launch traced here: 67.8 us
  Pallas kernels  66.1 us (97%)
  local copies, waits for them, and re-layouts  1.67 us (2%)
    pallas_call x1, Pallas kernels, fused(): pl.pallas_call(functools.partial(fused_kernel, row_count, local_heads, he...  66.1 us
    unnamed x1, local copies, waits for them, and re-layouts  1.67 us

profile of v1, /device:TPU:0, one launch (start us, length us, event | category | flops | bytes accessed | tf_op | source)
XLA Modules:
  0.0 67.8 jit_solution(7756854099576199462)
XLA Ops:
  0.0 66.1 %fused_attention.1 = bf16[32,4096]{1,0:T(8,128)(2,1)} custom-call(bf16[64,3072]{1,0:T(8,128)(2,1)} %tokens.1, bf16[3072,1536]{1,0:T(8,128)(2,1)} %w_qkv.1, f32[1,128]{1,0:T(1,128)} %bitcast.2, f32[1,128]{1,0:T(1,128)} %bitcast.3, f32[32]{0:T(128)} %logit_scale.1), custom_call_target="tpu_custom_call" | custom-call | tf_op jit(solution)/shard_map/fused_attention/pallas_call | solution.py:291
  66.1 1.7 %copy.7 = bf16[32,4096]{1,0:T(8,128)(2,1)} copy(bf16[32,4096]{1,0:T(8,128)(2,1)} %fused_attention.1) | data formatting | bytes 524288

commit v2 on v1

--- a/solution.py
+++ b/solution.py
@@ -11,6 +11,7 @@
 MESH = pl.DeviceIdType.MESH
 FAST = 2
 TILE = 256
+END_HOLD, MID_HOLD = 3, 4
 
 
 def visit_order(depth):
@@ -37,8 +38,8 @@
     heads = local_heads // 4
     span = heads * 3 * half_dim
     tok_rows = tokens.shape[0]
-    slab = FAST * tok_rows
     out_rows = tok_rows // 2
+    slab = FAST * out_rows
     order = visit_order(depth)
 
     row = lax.axis_index("row")
@@ -63,10 +64,19 @@
         )
 
     w_copies = [w_copy(c, far) for c in (other_col, col) for far in (0, 1)]
-    own_copy = pltpu.make_async_copy(
-        tokens, toks.at[pl.ds(pl.multiple_of(row * tok_rows, tok_rows), tok_rows)], own_sem
-    )
-    own_copy.start()
+    def chunk_at(at, xx, half):
+        start = ((at * 2 + half) * FAST + xx) * out_rows
+        return pl.ds(pl.multiple_of(start, out_rows), out_rows)
+
+    def own_half(half):
+        return tokens.at[pl.ds(half * out_rows, out_rows)]
+
+    own_copies = [
+        pltpu.make_async_copy(own_half(half), toks.at[chunk_at(z, x, half)], own_sem.at[half])
+        for half in (0, 1)
+    ]
+    for copy in own_copies + w_copies:
+        copy.start()
 
     barrier = pltpu.get_barrier_semaphore()
     for step in range(row_count):
@@ -81,29 +91,27 @@
             )
     pl.semaphore_wait(barrier, 2 * row_count - 1)
 
-    def block_at(block):
-        return toks.at[pl.ds(pl.multiple_of(block * tok_rows, tok_rows), tok_rows)]
-
-    def gather_copy(block, way, target, source=None):
+    def gather_copy(at, xx, half, way, target, source=None):
+        index = (at * FAST + xx) * 2 + half
+        place = toks.at[chunk_at(at, xx, half)]
         return pltpu.make_async_remote_copy(
-            src_ref=block_at(block) if source is None else source,
-            dst_ref=block_at(block),
-            send_sem=gather_send.at[way, block],
-            recv_sem=gather_recv.at[block],
+            src_ref=place if source is None else source,
+            dst_ref=place,
+            send_sem=gather_send.at[way, index],
+            recv_sem=gather_recv.at[index],
             device_id={"row": target},
             device_id_type=MESH,
         )
 
-    def column(distance, act):
+    def column(distance, half, act):
         for sign in (0,) if distance == 0 else (-1, 1):
             at = z + sign * distance
-            block = at * FAST + x
-            source = tokens if distance == 0 else None
+            source = own_half(half) if distance == 0 else None
 
             @pl.when(jnp.logical_and(at >= 0, at < depth))
             def _():
                 if act == "start" and distance:
-                    gather_copy(block, 0, across).wait_recv()
+                    gather_copy(at, x, half, 0, across).wait_recv()
 
                 def go(copy):
                     if act == "start":
@@ -115,38 +123,42 @@
 
                     @pl.when(z + 1 < depth)
                     def _():
-                        go(gather_copy(block, 1, row + FAST, source))
+                        go(gather_copy(at, x, half, 1, row + FAST, source))
 
                 if sign >= 0:
 
                     @pl.when(z >= 1)
                     def _():
-                        go(gather_copy(block, 2, row - FAST, source))
-
-                go(gather_copy(block, 0, across, source))
-
-    def part_copy(k):
+                        go(gather_copy(at, x, half, 2, row - FAST, source))
+
+                go(gather_copy(at, x, half, 0, across, source))
+
+    def part_copy(step):
         return pltpu.make_async_remote_copy(
-            src_ref=part_out.at[k], dst_ref=part_in.at[k],
-            send_sem=part_send.at[k], recv_sem=part_recv.at[k],
+            src_ref=part_out.at[step], dst_ref=part_in.at[step],
+            send_sem=part_send.at[step], recv_sem=part_recv.at[step],
             device_id={"col": other_col}, device_id_type=MESH,
         )
 
+    def batch_at(step):
+        return pick(z, [seq[step // 2] for seq in order]) * 2 + step % 2
+
     def slab_of(at):
         return pl.ds(pl.multiple_of(at * slab, slab), slab)
 
-    def cross_copy(k, at):
+    def cross_copy(step, at):
         return pltpu.make_async_remote_copy(
-            src_ref=crossing.at[k], dst_ref=joined.at[side, slab_of(at)],
-            send_sem=cross_send.at[k], recv_sem=cross_recv.at[at],
+            src_ref=crossing.at[step], dst_ref=joined.at[side, slab_of(at)],
+            send_sem=cross_send.at[step], recv_sem=cross_recv.at[at],
             device_id={"row": other_row}, device_id_type=MESH,
         )
 
-    def batch(k):
-        at = pick(z, [seq[k] for seq in order])
-        gather_copy(at * FAST + (1 - x), 0, across).wait_recv()
-        if k == 0:
-            own_copy.wait()
+    def batch(step):
+        at = batch_at(step)
+        gather_copy(pick(z, [seq[step // 2] for seq in order]), 1 - x, step % 2, 0, across).wait_recv()
+        if step < 2:
+            own_copies[step].wait()
+        if step == 0:
             for copy in w_copies:
                 copy.wait()
         rows = slab_of(at)
@@ -154,12 +166,12 @@
 
         @pl.loop(0, tiles)
         def _(n):
-            part_out[k, :, pl.ds(pl.multiple_of(n * TILE, TILE), TILE)] = jnp.dot(
+            part_out[step, :, pl.ds(pl.multiple_of(n * TILE, TILE), TILE)] = jnp.dot(
                 toks[rows, :], weights[:, pl.ds(pl.multiple_of(n * TILE, TILE), TILE)],
                 preferred_element_type=jnp.float32,
             )
 
-        part_copy(k).start()
+        part_copy(step).start()
 
         @pl.loop(0, tiles)
         def _(n):
@@ -168,19 +180,29 @@
                 preferred_element_type=jnp.float32,
             )
 
-        part_copy(k).wait_recv()
-        crossing[k] = (acc[:, span:] + part_in[k, :, span:]).astype(jnp.bfloat16)
-        cross_copy(k, at).start()
-        joined[side, rows, :] = (acc[:, :span] + part_in[k, :, :span]).astype(jnp.bfloat16)
-
-    column(0, "start")
-    for copy in w_copies:
-        copy.start()
-    column(1, "start")
-    for k in range(depth):
-        batch(k)
-        if k + 2 < depth:
-            column(k + 2, "start")
+        part_copy(step).wait_recv()
+        crossing[step] = (acc[:, span:] + part_in[step, :, span:]).astype(jnp.bfloat16)
+        for is_end, hold in ((True, END_HOLD), (False, MID_HOLD)):
+            first = min(hold, batches - 1)
+            ready = [step] if step > first else list(range(step + 1)) if step == first else []
+            if ready:
+
+                @pl.when(at_end if is_end else jnp.logical_not(at_end))
+                def _():
+                    for earlier in ready:
+                        cross_copy(earlier, batch_at(earlier)).start()
+
+        joined[side, rows, :] = (acc[:, :span] + part_in[step, :, :span]).astype(jnp.bfloat16)
+
+    at_end = jnp.logical_or(z == 0, z == depth - 1)
+    batches = 2 * depth
+    column(0, 0, "start")
+    column(0, 1, "start")
+    column(1, 0, "start")
+    for step in range(batches):
+        batch(step)
+        if step + 3 < batches:
+            column((step + 3) // 2, (step + 3) % 2, "start")
 
     lanes = lax.broadcasted_iota(jnp.int32, (slab, head_dim), 1)
     low = lanes < half_dim
@@ -213,8 +235,8 @@
                 kn[2 * j + i, rows, :] = normed(key, key_gain)
                 vv[2 * j + i, rows, :] = value.astype(jnp.bfloat16)
 
-    for k in range(depth):
-        prepare(pick(z, [seq[k] for seq in order]))
+    for step in range(batches):
+        prepare(batch_at(step))
 
     first_head = group * local_heads + (side * 2 + col) * heads
     out_cols = pl.ds(pl.multiple_of(first_head * head_dim, heads * head_dim), heads * head_dim)
@@ -222,30 +244,28 @@
 
     def out_copies(at, act):
         for xx in range(FAST):
-            for cc in (0, 1):
-                target = at * FAST + xx
-                source = att.at[
-                    pl.ds(pl.multiple_of(target * tok_rows + cc * out_rows, out_rows), out_rows)
-                ]
-                is_me = jnp.logical_and(target == row, col == cc)
-
-                @pl.when(is_me)
-                def _():
-                    copy = pltpu.make_async_copy(source, out.at[:, out_cols], self_sem)
-                    copy.start() if act == "start" else copy.wait()
-
-                @pl.when(jnp.logical_not(is_me))
-                def _():
-                    copy = pltpu.make_async_remote_copy(
-                        src_ref=source, dst_ref=out.at[:, out_cols],
-                        send_sem=out_send.at[target * 2 + cc], recv_sem=out_recv.at[me],
-                        device_id={"row": target, "col": jnp.int32(cc)}, device_id_type=MESH,
-                    )
-                    copy.start() if act == "start" else copy.wait_send()
+            target = at // 2 * FAST + xx
+            half = lax.rem(at, 2)
+            source = att.at[chunk_at(at // 2, xx, half)]
+            is_me = jnp.logical_and(target == row, col == half)
+
+            @pl.when(is_me)
+            def _():
+                copy = pltpu.make_async_copy(source, out.at[:, out_cols], self_sem)
+                copy.start() if act == "start" else copy.wait()
+
+            @pl.when(jnp.logical_not(is_me))
+            def _():
+                copy = pltpu.make_async_remote_copy(
+                    src_ref=source, dst_ref=out.at[:, out_cols],
+                    send_sem=out_send.at[target * 2 + half], recv_sem=out_recv.at[me],
+                    device_id={"row": target, "col": half}, device_id_type=MESH,
+                )
+                copy.start() if act == "start" else copy.wait_send()
 
     for k in reversed(range(depth)):
         at = pick(z, [seq[k] for seq in order])
-        rows = slab_of(at)
+        rows = pl.ds(pl.multiple_of(at * 2 * slab, 2 * slab), 2 * slab)
         for i in range(heads):
             scores = lax.dot_general(
                 qn[i, rows, :], kn[i], (((1,), (1,)), ((), ())), preferred_element_type=jnp.float32
@@ -255,15 +275,17 @@
             att[rows, i * head_dim:(i + 1) * head_dim] = jnp.dot(
                 probs, vv[i], preferred_element_type=jnp.float32
             ).astype(jnp.bfloat16)
-        out_copies(at, "start")
+        out_copies(at * 2, "start")
+        out_copies(at * 2 + 1, "start")
 
     for distance in range(depth):
-        column(distance, "finish")
-    for k in range(depth):
-        part_copy(k).wait_send()
-        cross_copy(k, pick(z, [seq[k] for seq in order])).wait_send()
-    for at in range(depth):
-        out_copies(at, "finish")
+        for half in (0, 1):
+            column(distance, half, "finish")
+    for step in range(batches):
+        part_copy(step).wait_send()
+        cross_copy(step, batch_at(step)).wait_send()
+    for at in range(batches):
+        out_copies(jnp.int32(at), "finish")
     for source in range(2 * row_count):
 
         @pl.when(source != me)
@@ -283,8 +305,8 @@
     span = w_qkv.shape[1] // 4
     tok_rows, width = tokens.shape
     count = tok_rows * row_count
-    depth = row_count // FAST
-    slab = FAST * tok_rows
+    batches = row_count // FAST * 2
+    slab = FAST * tok_rows // 2
     vmem, hbm = pl.BlockSpec(memory_space=pltpu.VMEM), pl.BlockSpec(memory_space=pl.ANY)
     dma = pltpu.SemaphoreType.DMA
     half = jnp.bfloat16
@@ -296,17 +318,17 @@
         scratch_shapes=[
             pltpu.VMEM((count, width), half),
             pltpu.VMEM(w_qkv.shape, half),
-            pltpu.VMEM((depth, slab, 2 * span), jnp.float32),
-            pltpu.VMEM((depth, slab, 2 * span), jnp.float32),
+            pltpu.VMEM((batches, slab, 2 * span), jnp.float32),
+            pltpu.VMEM((batches, slab, 2 * span), jnp.float32),
             pltpu.VMEM((slab, 2 * span), jnp.float32),
             pltpu.VMEM((2, count, span), half),
-            pltpu.VMEM((depth, slab, span), half),
+            pltpu.VMEM((batches, slab, span), half),
             pltpu.VMEM((heads, count, head_dim), half),
             pltpu.VMEM((heads, count, head_dim), half),
             pltpu.VMEM((heads, count, head_dim), half),
             pltpu.VMEM((count, heads * head_dim), half),
-            dma, dma((4,)), dma((3, row_count)), dma((row_count,)), dma((depth,)), dma((depth,)),
-            dma((depth,)), dma((depth,)), dma((2 * row_count,)), dma((2 * row_count,)), dma,
+            dma((2,)), dma((4,)), dma((3, 2 * row_count)), dma((2 * row_count,)), dma((batches,)),
+            dma((batches,)), dma((batches,)), dma((batches,)), dma((2 * row_count,)), dma((2 * row_count,)), dma,
         ],
         compiler_params=pltpu.CompilerParams(
             collective_id=0, has_side_effects=True, vmem_limit_bytes=60 * 2**20

time: 67.9 us -> 60.2 us (0.89)
  Pallas kernels: 66.1 us -> 58.3 us
    pallas_call x1, Pallas kernels: 66.1 us -> 58.3 us  [fused(): pl.pallas_call(functools.partial(fused_kernel, row_count, local_heads, he...]
where the time goes in v2:
time: 60.2 us; the launch traced here: 59.9 us
  Pallas kernels  58.3 us (97%)
  local copies, waits for them, and re-layouts  1.67 us (3%)
    pallas_call x1, Pallas kernels, fused(): pl.pallas_call(functools.partial(fused_kernel, row_count, local_heads, he...  58.3 us
    unnamed x1, local copies, waits for them, and re-layouts  1.67 us

profile of v2, /device:TPU:0, one launch (start us, length us, event | category | flops | bytes accessed | tf_op | source)
XLA Modules:
  0.0 59.9 jit_solution(4531834861678826735)
XLA Ops:
  0.0 58.3 %fused_attention.1 = bf16[32,4096]{1,0:T(8,128)(2,1)} custom-call(bf16[64,3072]{1,0:T(8,128)(2,1)} %tokens.1, bf16[3072,1536]{1,0:T(8,128)(2,1)} %w_qkv.1, f32[1,128]{1,0:T(1,128)} %bitcast.2, f32[1,128]{1,0:T(1,128)} %bitcast.3, f32[32]{0:T(128)} %logit_scale.1), custom_call_target="tpu_custom_call" | custom-call | tf_op jit(solution)/shard_map/fused_attention/pallas_call | solution.py:313
  58.3 1.7 %copy.7 = bf16[32,4096]{1,0:T(8,128)(2,1)} copy(bf16[32,4096]{1,0:T(8,128)(2,1)} %fused_attention.1) | data formatting | bytes 524288

commit v3 on v2

--- a/solution.py
+++ b/solution.py
@@ -79,17 +79,24 @@
         copy.start()
 
     barrier = pltpu.get_barrier_semaphore()
-    for step in range(row_count):
-        for c in (0, 1):
-            if step == 0 and c == 0:
-                continue
-            peer = lax.rem(row + step, row_count)
-            pl.semaphore_signal(
-                barrier, inc=1,
-                device_id={"row": peer, "col": col if c == 0 else other_col},
-                device_id_type=MESH,
-            )
-    pl.semaphore_wait(barrier, 2 * row_count - 1)
+    def greet(target):
+        pl.semaphore_signal(barrier, inc=1, device_id=target, device_id_type=MESH)
+
+    greet({"col": other_col})
+    greet({"row": across})
+    greet({"row": other_row})
+
+    @pl.when(z + 1 < depth)
+    def _():
+        greet({"row": row + FAST})
+
+    @pl.when(z >= 1)
+    def _():
+        greet({"row": row - FAST})
+
+    below = jnp.where(z >= 1, jnp.int32(1), jnp.int32(0))
+    above = jnp.where(z + 1 < depth, jnp.int32(1), jnp.int32(0))
+    pl.semaphore_wait(barrier, 3 + below + above)
 
     def gather_copy(at, xx, half, way, target, source=None):
         index = (at * FAST + xx) * 2 + half

time: 60.2 us -> 58.7 us (0.975)
  Pallas kernels: 58.3 us -> 56.9 us
    pallas_call x1, Pallas kernels: 58.3 us -> 56.9 us  [fused(): pl.pallas_call(functools.partial(fused_kernel, row_count, local_heads, he...]
where the time goes in v3:
time: 58.7 us; the launch traced here: 58.6 us
  Pallas kernels  56.9 us (97%)
  local copies, waits for them, and re-layouts  1.67 us (3%)
    pallas_call x1, Pallas kernels, fused(): pl.pallas_call(functools.partial(fused_kernel, row_count, local_heads, he...  56.9 us
    unnamed x1, local copies, waits for them, and re-layouts  1.67 us

profile of v3, /device:TPU:0, one launch (start us, length us, event | category | flops | bytes accessed | tf_op | source)
XLA Modules:
  0.0 58.6 jit_solution(16642567895134666725)
XLA Ops:
  0.0 56.9 %fused_attention.1 = bf16[32,4096]{1,0:T(8,128)(2,1)} custom-call(bf16[64,3072]{1,0:T(8,128)(2,1)} %tokens.1, bf16[3072,1536]{1,0:T(8,128)(2,1)} %w_qkv.1, f32[1,128]{1,0:T(1,128)} %bitcast.2, f32[1,128]{1,0:T(1,128)} %bitcast.3, f32[32]{0:T(128)} %logit_scale.1), custom_call_target="tpu_custom_call" | custom-call | tf_op jit(solution)/shard_map/fused_attention/pallas_call | solution.py:320
  56.9 1.7 %copy.7 = bf16[32,4096]{1,0:T(8,128)(2,1)} copy(bf16[32,4096]{1,0:T(8,128)(2,1)} %fused_attention.1) | data formatting | bytes 524288

commit v4 on v3

--- a/solution.py
+++ b/solution.py
@@ -11,7 +11,7 @@
 MESH = pl.DeviceIdType.MESH
 FAST = 2
 TILE = 256
-END_HOLD, MID_HOLD = 3, 4
+END_HOLD, MID_HOLD = 2, 3
 
 
 def visit_order(depth):
@@ -176,7 +176,7 @@
             part_out[step, :, pl.ds(pl.multiple_of(n * TILE, TILE), TILE)] = jnp.dot(
                 toks[rows, :], weights[:, pl.ds(pl.multiple_of(n * TILE, TILE), TILE)],
                 preferred_element_type=jnp.float32,
-            )
+            ).astype(jnp.bfloat16)
 
         part_copy(step).start()
 
@@ -325,8 +325,8 @@
         scratch_shapes=[
             pltpu.VMEM((count, width), half),
             pltpu.VMEM(w_qkv.shape, half),
-            pltpu.VMEM((batches, slab, 2 * span), jnp.float32),
-            pltpu.VMEM((batches, slab, 2 * span), jnp.float32),
+            pltpu.VMEM((batches, slab, 2 * span), half),
+            pltpu.VMEM((batches, slab, 2 * span), half),
             pltpu.VMEM((slab, 2 * span), jnp.float32),
             pltpu.VMEM((2, count, span), half),
             pltpu.VMEM((batches, slab, span), half),

time: 58.7 us -> 58.2 us (level)
  no operation moved by 1% of the time
where the time goes in v4:
time: 58.2 us; the launch traced here: 58.1 us
  Pallas kernels  56.4 us (97%)
  local copies, waits for them, and re-layouts  1.67 us (3%)
    pallas_call x1, Pallas kernels, fused(): pl.pallas_call(functools.partial(fused_kernel, row_count, local_heads, he...  56.4 us
    unnamed x1, local copies, waits for them, and re-layouts  1.67 us

profile of v4, /device:TPU:0, one launch (start us, length us, event | category | flops | bytes accessed | tf_op | source)
XLA Modules:
  0.0 58.1 jit_solution(4085296952248081515)
XLA Ops:
  0.0 56.4 %fused_attention.1 = bf16[32,4096]{1,0:T(8,128)(2,1)} custom-call(bf16[64,3072]{1,0:T(8,128)(2,1)} %tokens.1, bf16[3072,1536]{1,0:T(8,128)(2,1)} %w_qkv.1, f32[1,128]{1,0:T(1,128)} %bitcast.2, f32[1,128]{1,0:T(1,128)} %bitcast.3, f32[32]{0:T(128)} %logit_scale.1), custom_call_target="tpu_custom_call" | custom-call | tf_op jit(solution)/shard_map/fused_attention/pallas_call | solution.py:320
  56.4 1.7 %copy.7 = bf16[32,4096]{1,0:T(8,128)(2,1)} copy(bf16[32,4096]{1,0:T(8,128)(2,1)} %fused_attention.1) | data formatting | bytes 524288
